TPU v7x, 512 devices: a whole 4x8x8 slice. The times are simulated.
512 devices in a mesh: ctx: 32 (over z, y_lo), tp: 16 (over x, y_hi, core).
Axes of the slice: x: 4, y: 8 (y_hi: 2, y_lo: 4; y = y_hi * 4 + y_lo), z: 8, core: 2. Of those that a mesh axis runs over, the one named last changes fastest.
Arguments:
- queries: bfloat16 [4096, 6144], P('ctx', 'tp'), may hold values from -6 to 6
- keys: bfloat16 [4096, 6144], P('ctx', 'tp'), may hold values from -6 to 6
- values: bfloat16 [4096, 6144], P('ctx', 'tp'), may hold values from -6 to 6
- norm_gain: float32 [6144], P('tp'), may hold values from 0.1 to 1.9
- out_weight: bfloat16 [6144, 6144], P('tp', 'ctx'), may hold values from -0.15625 to 0.15625
Outputs:
- projected: bfloat16 [4096, 6144], P('ctx', 'tp')
All inputs are finite; a program needn't handle non-finite values.
Results may differ from a plain program's by a relative error of at most 0.017.
Values may be sent and summed in bfloat16 or wider, within the bound.
A program may use at most 64 MiB of HBM per device.

v0:
```python
import jax
import jax.numpy as jnp
from jax import lax
from jax.sharding import PartitionSpec as P

HS = 128


def prefix(x, axis, combine, identity):
    count, index = (lax.axis_size(axis), lax.axis_index(axis))
    everything = lax.all_gather(x.astype(jnp.bfloat16), axis)
    start = jnp.broadcast_to(jnp.asarray(identity, x.dtype), x.shape)

    def step(k, before):
        reached = k < index
        new = combine(before, everything[k].astype(x.dtype))
        return jnp.where(reached, new, before)

    return lax.fori_loop(0, count, step, start)


def add_states(earlier, later):
    return earlier + later


def carried_state(local_state):
    return prefix(local_state, "ctx", add_states, jnp.zeros_like(local_state))


def body(queries, keys, values, norm_gain, out_weight):
    tokens_here = queries.shape[0]
    features = queries.shape[1]
    heads_here = features // HS
    query_heads = queries.reshape(tokens_here, heads_here, HS)
    key_heads = keys.reshape(tokens_here, heads_here, HS)
    value_heads = values.reshape(tokens_here, heads_here, HS)
    local_state = jnp.einsum(
        "shd,she->hde", key_heads, value_heads, preferred_element_type=jnp.float32
    )
    scores = jnp.einsum("thd,shd->hts", query_heads, key_heads, preferred_element_type=jnp.float32)
    rows_index = lax.broadcasted_iota(jnp.int32, (tokens_here, tokens_here), 0)
    cols_index = lax.broadcasted_iota(jnp.int32, (tokens_here, tokens_here), 1)
    causal = rows_index >= cols_index
    scores = jnp.where(causal[None], scores, jnp.float32(0.0)).astype(jnp.bfloat16)
    within = jnp.einsum("hts,shd->thd", scores, value_heads, preferred_element_type=jnp.float32)
    prefix_state = carried_state(local_state)
    carried = jnp.einsum(
        "thd,hde->the",
        query_heads.astype(jnp.float32),
        prefix_state,
        precision=lax.Precision.HIGHEST,
    )
    mixed_sum = within + carried
    inverse_rms = lax.rsqrt(jnp.mean(mixed_sum * mixed_sum, axis=-1, keepdims=True) + 1e-06)
    attended = (mixed_sum * inverse_rms * norm_gain.reshape(heads_here, HS)).astype(jnp.bfloat16)
    attended = attended.reshape(tokens_here, features)
    partials = jnp.dot(
        attended,
        lax.all_gather(out_weight, "ctx", axis=1, tiled=True),
        preferred_element_type=jnp.float32,
    )
    return lax.psum_scatter(partials.astype(jnp.bfloat16), "tp", scatter_dimension=1, tiled=True)


def solution(mesh):
    return jax.shard_map(
        body,
        mesh=mesh,
        in_specs=(P("ctx", "tp"), P("ctx", "tp"), P("ctx", "tp"), P("tp"), P("tp", "ctx")),
        out_specs=P("ctx", "tp"),
        check_vma=False,
    )
```

profile of v0, /device:TPU:2, one launch (start us, length us, event | category | flops | bytes accessed | tf_op | source)
XLA Modules:
  0.0 449.8 jit_solution(4256987266796342964)
XLA Ops:
  6.5 0.0 copy-start
  6.5 0.0 all-gather.6.cloned.1.call-start
  6.5 1.0 copy.18
  7.6 1.0 copy.21
  8.6 0.8 convolution_convert_fusion.1
  9.4 0.0 all-gather.6.cloned.1.call-update
  9.4 0.0 all-gather.4.cloned.1.call-start
  9.5 0.7 all-gather.4.cloned.1.call-update
  10.2 0.0 reduce-scatter.4.cloned.1.call-start
  10.3 1.0 copy.17
  11.3 0.4 convolution_bitcast_fusion.1
  11.7 164.5 %all-gather.6.cloned.1.call-done = bf16[96,128,128]{2,1,0:T(8,128)(2,1)} async-done(((bf16[3,128,128]{2,1,0:T(8,128)(2,1)}), bf16[96,128,128]{2,1,0:T(8,128)(2,1)}) %all-gather.6.cloned.1.call-update) | async-done | bytes 3145744 | tf_op jit(solution)/shard_map/all_gather | solution.py:11
  176.2 32.3 %while.14 = (s32[]{:T(128)}, f32[3,128,128]{2,1,0:T(8,128)S(1)}, s32[]{:T(128)}, bf16[32,3,128,128]{3,2,1,0:T(8,128)(2,1)}, s32[]{:T(128)}, /*index=5*/s32[]{:T(128)}) while((s32[]{:T(128)}, f32[3,128,128]{2,1,0:T(8,128)S(1)}, s32[]{:T(128)}, bf16[32,3,128,128]{3,2,1,0:T(8,128)(2,1)}, s32[]{:T(128)}, /*index=5*/s32[]{:T(128)}) %tuple.42), condition=%wide.region_1.2_spmd.clone, body=%wide.region_0.1_spmd.clone.sunk | while | flops 196612 | bytes 491613 | solution.py:19
  176.2 1.0 add_select_fusion.2
  177.2 1.0 add_select_fusion.2
  178.2 1.0 add_select_fusion.2
  179.2 1.0 add_select_fusion.2
  180.2 1.0 add_select_fusion.2
  181.2 1.0 add_select_fusion.2
  182.2 1.0 add_select_fusion.2
  183.2 1.0 add_select_fusion.2
  184.3 1.0 add_select_fusion.2
  185.3 1.0 add_select_fusion.2
  186.3 1.0 add_select_fusion.2
  187.3 1.0 add_select_fusion.2
  188.3 1.0 add_select_fusion.2
  189.3 1.0 add_select_fusion.2
  190.3 1.0 add_select_fusion.2
  191.3 1.0 add_select_fusion.2
  192.3 1.0 add_select_fusion.2
  193.3 1.0 add_select_fusion.2
  194.3 1.0 add_select_fusion.2
  195.4 1.0 add_select_fusion.2
  196.4 1.0 add_select_fusion.2
  197.4 1.0 add_select_fusion.2
  198.4 1.0 add_select_fusion.2
  199.4 1.0 add_select_fusion.2
  200.4 1.0 add_select_fusion.2
  201.4 1.0 add_select_fusion.2
  202.4 1.0 add_select_fusion.2
  203.4 1.0 add_select_fusion.2
  204.4 1.0 add_select_fusion.2
  205.4 1.0 add_select_fusion.2
  206.5 1.0 add_select_fusion.2
  207.5 1.0 add_select_fusion.2
  208.5 0.4 multiply_reduce_fusion
  208.8 0.0 copy-done
  208.9 0.1 multiply_convert_fusion
  209.0 137.4 %all-gather.4.cloned.1.call-done = bf16[384,6144]{0,1:T(8,128)(2,1)} async-done(((bf16[384,192]{0,1:T(8,128)(2,1)}), bf16[384,6144]{0,1:T(8,128)(2,1)}) %all-gather.4.cloned.1.call-update) | async-done | bytes 4718608 | tf_op jit(solution)/shard_map/all_gather | solution.py:59
  346.4 4.0 convolution_convert_fusion
  350.4 1.6 copy.30
  352.0 0.0 reduce-scatter.4.cloned.1.call-update
  352.0 89.6 %reduce-scatter.4.cloned.1.call-done = bf16[384,128]{1,0:T(8,128)(2,1)} async-done(((bf16[6144,128]{1,0:T(8,128)(2,1)}), bf16[384,128]{1,0:T(8,128)(2,1)}) %reduce-scatter.4.cloned.1.call-update) | async-done | bytes 98320
  441.6 1.6 copy.31
  (3 shorter events, 0.0 us)
Async XLA Ops:
  6.5 202.3 %copy-start = (f32[384]{0:T(512)S(1)}, f32[384]{0:T(512)}, u32[]{:S(2)}) copy-start(f32[384]{0:T(512)} %param.10) | copy-start | bytes 4612
  6.5 169.7 %all-gather.6.cloned.1.call-start = ((), (), s32[]{:S(2)}) async-start(), calls=%async_computation.2 | async-start | bytes 3244032 | tf_op jit(solution)/shard_map/all_gather | solution.py:11
  9.4 337.0 %all-gather.4.cloned.1.call-start = ((), (), s32[]{:S(2)}) async-start(), calls=%async_computation.1 | async-start | bytes 4866048 | tf_op jit(solution)/shard_map/all_gather | solution.py:59
  10.2 431.4 %reduce-scatter.4.cloned.1.call-start = ((), (), s32[]{:S(2)}) async-start(), calls=%async_computation.3 | async-start | bytes 1671168
Sparse Core Ops, SparseCore 0:
  9.6 166.5 all-gather.5
  178.3 168.1 all-gather.3
  352.1 89.4 reduce-scatter.3
where the time goes:
time: 451 us; the launch traced here: 450 us
  waiting for transfers between devices  392 us (87%)
  other arithmetic  31.7 us (7%)
  between operations  13.2 us (3%)
  local copies, waits for them, and re-layouts  6.25 us (1%)
  matrix products  5.57 us (1%)
    all_gather x1, waiting for transfers between devices, prefix(): everything = lax.all_gather(x.astype(jnp.bfloat16), axis)  165 us
    all_gather x1, waiting for transfers between devices, body(): lax.all_gather(out_weight, 'ctx', axis=1, tiled=True)  137 us
    unnamed x4, waiting for transfers between devices  90.3 us
    select_n x32, other arithmetic, step(): return jnp.where(reached, new, before)  31.6 us
  transfers between devices with their start and end apart: 3, of which 3 were waited for; matrix products, arithmetic and copies ran while one was open for 7% of the time, Pallas kernels for 0%

commit v1 on v0

--- a/solution.py
+++ b/solution.py
@@ -56,7 +56,9 @@
     attended = attended.reshape(tokens_here, features)
     partials = jnp.dot(
         attended,
-        lax.all_gather(out_weight, "ctx", axis=1, tiled=True),
+        jnp.concatenate(
+            lax.all_to_all(jnp.stack([out_weight] * lax.axis_size("ctx")), "ctx", 0, 0), axis=1
+        ),
         preferred_element_type=jnp.float32,
     )
     return lax.psum_scatter(partials.astype(jnp.bfloat16), "tp", scatter_dimension=1, tiled=True)

time: 451 us -> 392 us (0.87)
  waiting for transfers between devices: 392 us -> 316 us
  starting transfers between devices: 0.08 us -> 14 us
    all_gather x1 -> x0, waiting for transfers between devices: 137 us -> none  [body(): lax.all_gather(out_weight, 'ctx', axis=1, tiled=True)]
    all_gather x1, waiting for transfers between devices: 165 us -> 207 us  [prefix(): everything = lax.all_gather(x.astype(jnp.bfloat16), axis)]
    unnamed x4 -> x3, waiting for transfers between devices: 90.3 us -> 109 us
    all_to_all x0 -> x1, starting transfers between devices: none -> 14 us  [body(): lax.all_to_all(jnp.stack([out_weight] * lax.axis_size('ctx')), 'ctx', 0, 0)]
  transfers between devices with their start and end apart: 3 -> 3, of which waited for: 3 -> 2; matrix products, arithmetic and copies ran while one was open for 7% -> 9% of each run, Pallas kernels for 0% -> 0%
where the time goes in v1:
time: 392 us; the launch traced here: 391 us
  waiting for transfers between devices  316 us (81%)
  other arithmetic  31.7 us (8%)
  starting transfers between devices  14 us (4%)
  between operations  13.5 us (3%)
  local copies, waits for them, and re-layouts  9.15 us (2%)
  matrix products  5.53 us (1%)
    all_gather x1, waiting for transfers between devices, prefix(): everything = lax.all_gather(x.astype(jnp.bfloat16), axis)  207 us
    unnamed x3, waiting for transfers between devices  109 us
    select_n x32, other arithmetic, step(): return jnp.where(reached, new, before)  31.6 us
    all_to_all x1, starting transfers between devices, body(): lax.all_to_all(jnp.stack([out_weight] * lax.axis_size('ctx')), 'ctx', 0, 0)  14 us
  transfers between devices with their start and end apart: 3, of which 2 were waited for; matrix products, arithmetic and copies ran while one was open for 9% of the time, Pallas kernels for 0%

profile of v1, /device:TPU:2, one launch (start us, length us, event | category | flops | bytes accessed | tf_op | source)
XLA Modules:
  0.0 390.9 jit_solution(8363685247034319548)
XLA Ops:
  6.5 0.0 all-gather.3.cloned.1.call-start
  6.5 1.0 copy.19
  7.5 1.0 copy.22
  8.6 0.8 convolution_convert_fusion.1
  9.4 0.0 all-gather.3.cloned.1.call-update
  9.4 3.8 stack.2
  13.2 0.0 copy-start
  13.2 14.0 %all-to-all-start = ((bf16[32,384,192]{1,2,0:T(8,128)(2,1)}), bf16[32,384,192]{1,2,0:T(8,128)(2,1)}, u32[]{:S(2)}, u32[]{:S(2)}) async-start(bf16[32,384,192]{1,2,0:T(8,128)(2,1)} %stack.2), calls=%async_computation | async-start | bytes 9437184 | tf_op jit(solution)/shard_map/all_to_all | solution.py:60
  27.2 0.0 copy-start.1
  27.2 0.0 reduce-scatter.4.cloned.1.call-start
  27.3 0.0 copy-done
  27.3 0.1 copy.18
  27.5 0.4 convolution_bitcast_fusion.1
  27.9 206.9 %all-gather.3.cloned.1.call-done = bf16[96,128,128]{2,1,0:T(8,128)(2,1)} async-done(((bf16[3,128,128]{2,1,0:T(8,128)(2,1)}), bf16[96,128,128]{2,1,0:T(8,128)(2,1)}) %all-gather.3.cloned.1.call-update) | async-done | bytes 3145744 | tf_op jit(solution)/shard_map/all_gather | solution.py:11
  234.8 32.3 %while.14 = (s32[]{:T(128)}, f32[3,128,128]{2,1,0:T(8,128)S(1)}, s32[]{:T(128)}, bf16[32,3,128,128]{3,2,1,0:T(8,128)(2,1)}, s32[]{:T(128)}, /*index=5*/s32[]{:T(128)}) while((s32[]{:T(128)}, f32[3,128,128]{2,1,0:T(8,128)S(1)}, s32[]{:T(128)}, bf16[32,3,128,128]{3,2,1,0:T(8,128)(2,1)}, s32[]{:T(128)}, /*index=5*/s32[]{:T(128)}) %tuple.40), condition=%wide.region_1.2_spmd.clone, body=%wide.region_0.1_spmd.clone.sunk | while | flops 196612 | bytes 491621 | solution.py:19
  234.8 1.0 add_select_fusion.2
  235.8 1.0 add_select_fusion.2
  236.8 1.0 add_select_fusion.2
  237.8 1.0 add_select_fusion.2
  238.8 1.0 add_select_fusion.2
  239.8 1.0 add_select_fusion.2
  240.8 1.0 add_select_fusion.2
  241.9 1.0 add_select_fusion.2
  242.9 1.0 add_select_fusion.2
  243.9 1.0 add_select_fusion.2
  244.9 1.0 add_select_fusion.2
  245.9 1.0 add_select_fusion.2
  246.9 1.0 add_select_fusion.2
  247.9 1.0 add_select_fusion.2
  248.9 1.0 add_select_fusion.2
  249.9 1.0 add_select_fusion.2
  250.9 1.0 add_select_fusion.2
  251.9 1.0 add_select_fusion.2
  253.0 1.0 add_select_fusion.2
  254.0 1.0 add_select_fusion.2
  255.0 1.0 add_select_fusion.2
  256.0 1.0 add_select_fusion.2
  257.0 1.0 add_select_fusion.2
  258.0 1.0 add_select_fusion.2
  259.0 1.0 add_select_fusion.2
  260.0 1.0 add_select_fusion.2
  261.0 1.0 add_select_fusion.2
  262.0 1.0 add_select_fusion.2
  263.0 1.0 add_select_fusion.2
  264.1 1.0 add_select_fusion.2
  265.1 1.0 add_select_fusion.2
  266.1 1.0 add_select_fusion.2
  267.1 0.4 multiply_reduce_fusion
  267.4 0.0 copy-done.1
  267.5 0.1 multiply_convert_fusion
  267.6 0.0 all-to-all-done
  267.6 3.9 %convolution_convert_fusion = bf16[128,6144]{1,0:T(8,128)(2,1)S(1)} fusion(bf16[128,384]{0,1:T(8,128)(2,1)S(1)} %bitcast.38, bf16[384,6144]{0,1:T(8,128)(2,1)} %bitcast.9), kind=kOutput, calls=%fused_computation.1 | convolution fusion | flops 604766208 | bytes 6389760 | tf_op jit(solution)/shard_map/dot_general | solution.py:57
  271.5 1.6 copy.31
  273.1 0.0 reduce-scatter.4.cloned.1.call-update
  273.1 109.3 %reduce-scatter.4.cloned.1.call-done = bf16[384,128]{1,0:T(8,128)(2,1)} async-done(((bf16[6144,128]{1,0:T(8,128)(2,1)}), bf16[384,128]{1,0:T(8,128)(2,1)}) %reduce-scatter.4.cloned.1.call-update) | async-done | bytes 98320
  382.5 1.6 copy.32
  (3 shorter events, 0.0 us)
Async XLA Ops:
  6.5 228.3 %all-gather.3.cloned.1.call-start = ((), (), s32[]{:S(2)}) async-start(), calls=%async_computation.2 | async-start | bytes 3244032 | tf_op jit(solution)/shard_map/all_gather | solution.py:11
  13.2 14.1 %copy-start = (bf16[128,384]{1,0:T(8,128)(2,1)S(1)}, bf16[128,384]{1,0:T(8,128)(2,1)}, u32[]{:S(2)}) copy-start(bf16[128,384]{1,0:T(8,128)(2,1)} %param.7) | copy-start | bytes 294916
  13.2 254.4 %all-to-all-start = ((bf16[32,384,192]{1,2,0:T(8,128)(2,1)}), bf16[32,384,192]{1,2,0:T(8,128)(2,1)}, u32[]{:S(2)}, u32[]{:S(2)}) async-start(bf16[32,384,192]{1,2,0:T(8,128)(2,1)} %stack.2), calls=%async_computation | async-start | bytes 9437184 | tf_op jit(solution)/shard_map/all_to_all | solution.py:60
  27.2 240.2 %copy-start.1 = (f32[384]{0:T(512)S(1)}, f32[384]{0:T(512)}, u32[]{:S(2)}) copy-start(f32[384]{0:T(512)} %param.10) | copy-start | bytes 4612
  27.2 355.2 %reduce-scatter.4.cloned.1.call-start = ((), (), s32[]{:S(2)}) async-start(), calls=%async_computation.3 | async-start | bytes 1671168
Sparse Core Ops, SparseCore 0:
  9.6 225.2 all-gather.2
  273.2 109.1 reduce-scatter.3
